TPU v7x, 256 devices: a whole 4x4x8 slice. The times are simulated.
256 devices in a mesh: seq: 32 (over y, x, core), head: 8 (over z).
Axes of the slice: x: 4, y: 4, z: 8, core: 2. Of those that a mesh axis runs over, the one named last changes fastest.
Arguments:
- query_rows: bfloat16 [16384, 4096], P('seq', 'head'), may hold values from -6 to 6
- key_rows: bfloat16 [16384, 4096], P('seq', 'head'), may hold values from -6 to 6
- value_rows: bfloat16 [16384, 4096], P('seq', 'head'), may hold values from -6 to 6
- out_weight: bfloat16 [4096, 4096], P('seq', 'head'), may hold values from -0.09375 to 0.09375
- target_rows: bfloat16 [16384, 4096], P('seq', 'head'), may hold values from -6 to 6
Outputs:
- output: bfloat16 [16384, 4096], P('seq', 'head')
- grad_query: bfloat16 [16384, 4096], P('seq', 'head')
- grad_key: bfloat16 [16384, 4096], P('seq', 'head')
- grad_value: bfloat16 [16384, 4096], P('seq', 'head')
- grad_weight: float32 [4096, 4096], P('seq', 'head')
All inputs are finite; a program needn't handle non-finite values.
Results may differ from a plain program's by a relative error of at most 0.019.
Values may be sent and summed in bfloat16 or wider, within the bound.
A program may use at most 64 MiB of HBM per device.

v0:
```python
import math
import jax
import jax.numpy as jnp
from jax import lax
from jax.sharding import Mesh
from jax.sharding import PartitionSpec as P

DH = 128
BLK = 512
SEQ = ("seq_0", "seq_1", "seq_2")
EXACT = lax.Precision.HIGHEST


def filled_with(x, identity):
    return jnp.broadcast_to(jnp.asarray(identity, x.dtype), x.shape)


def entering(x, axes, combine, identity, reverse):
    before = start = filled_with(x, identity)
    so_far = x
    for axis in reversed(axes):
        devices, place = (lax.axis_size(axis), lax.axis_index(axis))
        pieces = lax.all_gather(so_far.astype(jnp.bfloat16), axis)
        inside, so_far = (start, start)
        for k in reversed(range(devices)) if reverse else range(devices):
            passed = k > place if reverse else k < place
            so_far = combine(so_far, pieces[k].astype(x.dtype))
            inside = jnp.where(passed, so_far, inside)
        before = combine(inside, before)
    return before


def add_states(earlier, later_one):
    return earlier + later_one


def on_device(query_rows, key_rows, value_rows, out_weight, target_rows):
    rows_dev = query_rows.shape[0]
    feature_width = query_rows.shape[1]
    local_heads = feature_width // DH
    block_count = rows_dev // BLK
    seq_count = lax.axis_size(SEQ)
    total_rows = rows_dev * seq_count
    seq_index = lax.axis_index(SEQ)
    positions = (seq_index * rows_dev + jnp.arange(rows_dev, dtype=jnp.int32) + 1).astype(
        jnp.float32
    )
    query_scale = lax.rsqrt(jnp.float32(DH) * positions)
    scaled = (query_rows.astype(jnp.float32) * query_scale[:, None]).astype(jnp.bfloat16)
    shaped = (block_count, BLK, local_heads, DH)
    query_blocks = scaled.reshape(shaped)
    key_blocks = key_rows.reshape(shaped)
    value_blocks = value_rows.reshape(shaped)
    causal = jnp.tril(jnp.ones((BLK, BLK), dtype=bool))
    empty_state = jnp.zeros((local_heads, DH, DH), jnp.float32)
    block_kv = jnp.einsum(
        "bshd,bshe->bhde", key_blocks, value_blocks, preferred_element_type=jnp.float32
    )
    local_total = jnp.sum(block_kv, axis=0)
    earlier = entering(local_total, SEQ, add_states, empty_state, False)
    running_kv = jnp.cumsum(block_kv, axis=0)
    before = earlier[None] + jnp.concatenate([jnp.zeros_like(block_kv), running_kv[:-1]], axis=0)
    inter = jnp.einsum("bthd,bhde->bthe", query_blocks.astype(jnp.float32), before, precision=EXACT)
    scores = jnp.einsum(
        "bthd,bshd->bhts", query_blocks, key_blocks, preferred_element_type=jnp.float32
    )
    scores = jnp.where(causal, scores, 0.0).astype(jnp.bfloat16)
    intra = jnp.einsum("bhts,bshe->bthe", scores, value_blocks, preferred_element_type=jnp.float32)
    attended = (inter + intra).astype(jnp.bfloat16).reshape(rows_dev, feature_width)
    whole_weight = lax.all_gather(out_weight, SEQ, axis=0, tiled=True)
    partial_out = lax.dot_general(
        attended, whole_weight, (((1,), (1,)), ((), ())), preferred_element_type=jnp.float32
    )
    summed = lax.psum_scatter(
        partial_out.astype(jnp.bfloat16), "head", scatter_dimension=1, tiled=True
    )
    residual = (summed.astype(jnp.float32) - target_rows.astype(jnp.float32)).astype(jnp.bfloat16)
    residual_full = lax.all_gather(residual, "head", axis=1, tiled=True)
    grad_attended = jnp.dot(residual_full, whole_weight, preferred_element_type=jnp.float32).astype(
        jnp.bfloat16
    )
    weight_factor = 1.0 / math.sqrt(total_rows)
    product = lax.dot_general(
        residual_full, attended, (((0,), (0,)), ((), ())), preferred_element_type=jnp.float32
    )
    grad_weight = lax.psum_scatter(
        (product * weight_factor).astype(jnp.bfloat16), SEQ, scatter_dimension=0, tiled=True
    ).astype(jnp.float32)
    grad_blocks = grad_attended.reshape(shaped)
    block_qg = jnp.einsum(
        "bthd,bthe->bhde", query_blocks, grad_blocks, preferred_element_type=jnp.float32
    )
    local_grad = jnp.sum(block_qg, axis=0)
    later = entering(local_grad, SEQ, add_states, empty_state, True)
    running_qg = jnp.cumsum(block_qg[::-1], axis=0)[::-1]
    after = later[None] + jnp.concatenate([running_qg[1:], jnp.zeros_like(block_qg)], axis=0)
    mixed = jnp.einsum(
        "bthe,bshe->bhts", grad_blocks, value_blocks, preferred_element_type=jnp.float32
    )
    mixed = jnp.where(causal, mixed, 0.0).astype(jnp.bfloat16)
    grad_scaled = jnp.einsum(
        "bthe,bhde->bthd", grad_blocks.astype(jnp.float32), before, precision=EXACT
    )
    grad_scaled = grad_scaled + jnp.einsum(
        "bhts,bshd->bthd", mixed, key_blocks, preferred_element_type=jnp.float32
    )
    grad_key = jnp.einsum(
        "bshe,bhde->bshd", value_blocks.astype(jnp.float32), after, precision=EXACT
    )
    grad_key = grad_key + jnp.einsum(
        "bhts,bthd->bshd", mixed, query_blocks, preferred_element_type=jnp.float32
    )
    grad_value = jnp.einsum(
        "bshd,bhde->bshe", key_blocks.astype(jnp.float32), after, precision=EXACT
    )
    grad_value = grad_value + jnp.einsum(
        "bhts,bthe->bshe", scores, grad_blocks, preferred_element_type=jnp.float32
    )
    grad_query = (grad_scaled.reshape(rows_dev, feature_width) * query_scale[:, None]).astype(
        jnp.bfloat16
    )
    return (
        summed,
        grad_query,
        grad_key.astype(jnp.bfloat16).reshape(rows_dev, feature_width),
        grad_value.astype(jnp.bfloat16).reshape(rows_dev, feature_width),
        grad_weight,
    )


def solution(mesh):
    torus = Mesh(
        mesh.devices.reshape(4, 4, 2, mesh.shape["head"]), ("seq_0", "seq_1", "seq_2", "head")
    )
    return jax.shard_map(
        on_device,
        mesh=torus,
        in_specs=(P(SEQ, "head"), P(SEQ, "head"), P(SEQ, "head"), P(SEQ, "head"), P(SEQ, "head")),
        out_specs=(P(SEQ, "head"), P(SEQ, "head"), P(SEQ, "head"), P(SEQ, "head"), P(SEQ, "head")),
        check_vma=False,
    )
```

profile of v0, /device:TPU:2, one launch (start us, length us, event | category | flops | bytes accessed | tf_op | source)
XLA Modules:
  0.0 285.8 jit_solution(8579663501388462409)
XLA Ops:
  7.2 0.0 copy-start
  7.2 0.0 all-gather.5.cloned.1.call-start
  7.2 0.7 all-gather.5.cloned.1.call-update
  7.9 0.0 reduce-scatter.3.cloned.1.call-start
  8.0 1.3 copy.82
  9.3 1.4 multiply_convert_fusion.2
  10.7 0.2 copy.55
  10.9 0.3 convolution_convert_fusion.3
  11.2 2.0 all-gather
  13.2 0.1 iota_compare_fusion
  13.3 12.8 %all_gather.31 = bf16[4,4,128,128]{3,2,1,0:T(8,128)(2,1)S(1)} all-gather(bf16[1,4,128,128]{3,2,1,0:T(8,128)(2,1)S(1)} %fusion.41), channel_id=1, replica_groups=mesh['seq_0'=4,'seq_1'=4,'seq_2'=2,'head'=8] {'seq_1'}, dimensions={0}, use_global_device_ids=true | all-gather | bytes 655360 | tf_op jit(solution)/shard_map/all_gather | solution.py:23
  26.2 0.1 fusion.40
  26.2 15.3 %all_gather.32 = bf16[4,4,128,128]{3,2,1,0:T(8,128)(2,1)S(1)} all-gather(bf16[1,4,128,128]{3,2,1,0:T(8,128)(2,1)S(1)} %fusion.40), channel_id=1, replica_groups=mesh['seq_0'=4,'seq_1'=4,'seq_2'=2,'head'=8] {'seq_0'}, dimensions={0}, use_global_device_ids=true | all-gather | bytes 655360 | tf_op jit(solution)/shard_map/all_gather | solution.py:23
  41.6 0.3 fusion.20
  41.8 2.0 select_convert_fusion.1
  43.8 0.8 convolution_bitcast_fusion.1
  44.7 1.4 fusion
  46.1 18.6 %all-gather.5.cloned.1.call-done = bf16[4096,512]{1,0:T(8,128)(2,1)} async-done(((bf16[128,512]{1,0:T(8,128)(2,1)}), bf16[4096,512]{1,0:T(8,128)(2,1)}) %all-gather.5.cloned.1.call-update) | async-done | bytes 4194320 | tf_op jit(solution)/shard_map/all_gather | solution.py:70
  64.7 6.7 %convolution_convert_fusion = bf16[512,4096]{1,0:T(8,128)(2,1)} fusion(bf16[512,512]{0,1:T(8,128)(2,1)} %bitcast.114, bf16[4096,512]{1,0:T(8,128)(2,1)} %all-gather.5.cloned.1.call-done), kind=kOutput, calls=%fused_computation.1 | convolution fusion | flops 2149580800 | bytes 8912896 | tf_op jit(solution)/shard_map/dot_general | solution.py:71
  71.5 0.0 reduce-scatter.3.cloned.1.call-update
  71.5 0.0 all-gather.7.cloned.1.call-start
  71.5 55.2 %reduce-scatter.3.cloned.1.call-done = bf16[512,512]{1,0:T(8,128)(2,1)} async-done(((bf16[512,4096]{1,0:T(8,128)(2,1)}), bf16[512,512]{1,0:T(8,128)(2,1)}) %reduce-scatter.3.cloned.1.call-update) | async-done | bytes 524304 | tf_op jit(solution)/shard_map/reduce_scatter | solution.py:74
  126.7 2.1 subtract_convert_fusion
  128.9 0.0 all-gather.7.cloned.1.call-update
  128.9 0.0 reduce-scatter.5.cloned.1.call-start
  128.9 53.6 %all-gather.7.cloned.1.call-done = bf16[512,4096]{1,0:T(8,128)(2,1)} async-done(((bf16[512,512]{1,0:T(8,128)(2,1)}), bf16[512,4096]{1,0:T(8,128)(2,1)}) %all-gather.7.cloned.1.call-update) | async-done | bytes 4194320 | tf_op jit(solution)/shard_map/all_gather | solution.py:78
  182.5 6.7 %multiply_convert_fusion = bf16[4096,512]{1,0:T(8,128)(2,1)} fusion(bf16[512,4096]{1,0:T(8,128)(2,1)} %all-gather.7.cloned.1.call-done, bf16[512,512]{0,1:T(8,128)(2,1)} %bitcast.115), kind=kOutput, calls=%fused_computation | convolution fusion | flops 2151677952 | bytes 8912896 | tf_op jit(solution)/shard_map/dot_general | solution.py:83
  189.2 0.0 reduce-scatter.5.cloned.1.call-update
  189.3 5.8 %convolution_convert_fusion.1 = bf16[512,512]{0,1:T(8,128)(2,1)S(1)} fusion(bf16[512,4096]{1,0:T(8,128)(2,1)} %all-gather.7.cloned.1.call-done, bf16[4096,512]{1,0:T(8,128)(2,1)} %all-gather.5.cloned.1.call-done), kind=kOutput, calls=%fused_computation.10 | convolution fusion | flops 2147745792 | bytes 8912896 | tf_op jit(solution)/shard_map/dot_general | solution.py:79
  195.1 0.3 convolution_convert_fusion.2
  195.4 2.1 all-gather.1
  197.6 13.5 %all_gather.36 = bf16[4,4,128,128]{3,2,1,0:T(8,128)(2,1)S(1)} all-gather(bf16[1,4,128,128]{3,2,1,0:T(8,128)(2,1)S(1)} %fusion.42), channel_id=1, replica_groups=mesh['seq_0'=4,'seq_1'=4,'seq_2'=2,'head'=8] {'seq_1'}, dimensions={0}, use_global_device_ids=true | all-gather | bytes 655360 | tf_op jit(solution)/shard_map/all_gather | solution.py:23
  211.1 0.1 fusion.39
  211.2 13.5 %all_gather.37 = bf16[4,4,128,128]{3,2,1,0:T(8,128)(2,1)S(1)} all-gather(bf16[1,4,128,128]{3,2,1,0:T(8,128)(2,1)S(1)} %fusion.39), channel_id=1, replica_groups=mesh['seq_0'=4,'seq_1'=4,'seq_2'=2,'head'=8] {'seq_0'}, dimensions={0}, use_global_device_ids=true | all-gather | bytes 655360 | tf_op jit(solution)/shard_map/all_gather | solution.py:23
  224.7 0.3 fusion.29
  224.9 0.4 fusion.44
  225.4 0.6 fusion.2
  226.0 1.0 copy.49
  227.0 1.9 select_convert_fusion
  229.0 0.4 fusion.43
  229.4 1.4 fusion.1
  230.8 2.1 copy.48
  232.9 1.8 convolution_bitcast_fusion
  234.8 0.6 convolution_add_fusion.2
  235.4 0.3 copy.41
  235.7 0.9 multiply_convert_fusion.1
  236.7 41.0 %reduce-scatter.5.cloned.1.call-done = bf16[128,512]{1,0:T(8,128)(2,1)} async-done(((bf16[4096,512]{1,0:T(8,128)(2,1)}), bf16[128,512]{1,0:T(8,128)(2,1)}) %reduce-scatter.5.cloned.1.call-update) | async-done | bytes 131088 | tf_op jit(solution)/shard_map/reduce_scatter | solution.py:86
  277.6 1.6 convert_element_type.247
  (18 shorter events, 0.1 us)
Async XLA Ops:
  7.2 3.7 %copy-start = (bf16[512,512]{1,0:T(8,128)(2,1)S(1)}, bf16[512,512]{1,0:T(8,128)(2,1)}, u32[]{:S(2)}) copy-start(bf16[512,512]{1,0:T(8,128)(2,1)} %param.7) | copy-start | bytes 1572868
  7.2 57.6 %all-gather.5.cloned.1.call-start = ((), (), s32[]{:S(2)}) async-start(), calls=%async_computation.2 | async-start | bytes 4325376 | tf_op jit(solution)/shard_map/all_gather | solution.py:70
  7.9 118.8 %reduce-scatter.3.cloned.1.call-start = ((), (), s32[]{:S(2)}) async-start(), calls=%async_computation.3 | async-start | bytes 4718592 | tf_op jit(solution)/shard_map/reduce_scatter | solution.py:74
  9.2 32.6 %copy-start.5 = (bf16[512,512]{0,1:T(8,128)(2,1)}, bf16[512,512]{0,1:T(8,128)(2,1)S(1)}, u32[]{:S(2)}) copy-start(bf16[512,512]{0,1:T(8,128)(2,1)S(1)} %copy.82) | copy-start | bytes 1572868
  13.3 31.4 %copy-start.7 = (pred[512,512]{1,0:T(8,128)(4,1)}, pred[512,512]{1,0:T(8,128)(4,1)S(1)}, u32[]{:S(2)}) copy-start(pred[512,512]{1,0:T(8,128)(4,1)S(1)} %iota_compare_fusion) | copy-start | bytes 786436
  41.8 2.8 copy-start.3
  71.5 111.0 %all-gather.7.cloned.1.call-start = ((), (), s32[]{:S(2)}) async-start(), calls=%async_computation.4 | async-start | bytes 4718592 | tf_op jit(solution)/shard_map/all_gather | solution.py:78
  128.9 148.8 %reduce-scatter.5.cloned.1.call-start = ((), (), s32[]{:S(2)}) async-start(), calls=%async_computation.5 | async-start | bytes 4325376 | tf_op jit(solution)/shard_map/reduce_scatter | solution.py:86
  195.1 30.3 %copy-start.1 = (bf16[512,512]{0,1:T(8,128)(2,1)}, bf16[512,512]{0,1:T(8,128)(2,1)S(1)}, u32[]{:S(2)}) copy-start(bf16[512,512]{0,1:T(8,128)(2,1)S(1)} %convolution_convert_fusion.1) | copy-start | bytes 1572868
  195.4 30.0 %copy-start.6 = (bf16[512,512]{1,0:T(8,128)(2,1)S(1)}, bf16[512,512]{1,0:T(8,128)(2,1)}, u32[]{:S(2)}) copy-start(bf16[512,512]{1,0:T(8,128)(2,1)} %param.6) | copy-start | bytes 1572868
  229.4 5.3 %copy-start.2 = (bf16[512,512]{0,1:T(8,128)(2,1)S(1)}, bf16[512,512]{0,1:T(8,128)(2,1)}, u32[]{:S(2)}) copy-start(bf16[512,512]{0,1:T(8,128)(2,1)} %copy-done.1) | copy-start | bytes 1572868
  230.8 4.0 %copy-start.4 = (f32[4,128,128]{2,1,0:T(8,128)S(1)}, f32[4,128,128]{2,1,0:T(8,128)}, u32[]{:S(2)}) copy-start(f32[4,128,128]{2,1,0:T(8,128)} %copy-done.3) | copy-start | bytes 786436
Sparse Core Ops, SparseCore 0:
  10.5 54.1 all-gather.4
  71.6 55.0 reduce-scatter.2
  129.1 53.3 all-gather.6
  189.3 88.2 reduce-scatter.4
where the time goes:
time: 286 us
  waiting for transfers between devices  169 us (59%)
  blocking collectives  59.3 us (21%)
  matrix products  31.3 us (11%)
  between operations  14.1 us (5%)
  other arithmetic  6.88 us (2%)
  local copies, waits for them, and re-layouts  4.94 us (2%)
    all_gather x6, blocking collectives, entering(): pieces = lax.all_gather(so_far.astype(jnp.bfloat16), axis)  59.3 us
    reduce_scatter x1, waiting for transfers between devices, on_device(): lax.psum_scatter(partial_out.astype(jnp.bfloat16), 'head', scatter_dimens...  55.2 us
    all_gather x1, waiting for transfers between devices, on_device(): residual_full = lax.all_gather(residual, 'head', axis=1, tiled=True)  53.6 us
    reduce_scatter x1, waiting for transfers between devices, on_device(): lax.psum_scatter((product * weight_factor).astype(jnp.bfloat16), SEQ, sca...  41 us
    all_gather x1, waiting for transfers between devices, on_device(): whole_weight = lax.all_gather(out_weight, SEQ, axis=0, tiled=True)  18.6 us
    dot_general x1, matrix products, on_device(): lax.dot_general(attended, whole_weight, (((1,), (1,)), ((), ())), preferr...  6.73 us
    dot_general x1, matrix products, on_device(): lax.dot_general(residual_full, attended, (((0,), (0,)), ((), ())), prefer...  6.68 us
    dot_general x1, matrix products, on_device(): jnp.dot(residual_full, whole_weight, preferred_element_type=jnp.float32)  5.84 us
  transfers between devices with their start and end apart: 4, of which 4 were waited for; matrix products, arithmetic and copies ran while one was open for 9% of the time, Pallas kernels for 0%

commit v1 on v0

--- a/solution.py
+++ b/solution.py
@@ -75,7 +75,9 @@
         partial_out.astype(jnp.bfloat16), "head", scatter_dimension=1, tiled=True
     )
     residual = (summed.astype(jnp.float32) - target_rows.astype(jnp.float32)).astype(jnp.bfloat16)
-    residual_full = lax.all_gather(residual, "head", axis=1, tiled=True)
+    f_now = jnp.stack([residual] * lax.axis_size("head"), 0)
+    g_now = lax.all_to_all(f_now, "head", 0, 0)
+    residual_full = jnp.concatenate(g_now, 1)
     grad_attended = jnp.dot(residual_full, whole_weight, preferred_element_type=jnp.float32).astype(
         jnp.bfloat16
     )

time: 286 us -> 334 us (1.17)
  blocking collectives: 59.3 us -> 160 us
  waiting for transfers between devices: 169 us -> 113 us
  local copies, waits for them, and re-layouts: 4.94 us -> 10.4 us
    all_to_all x0 -> x1, blocking collectives: none -> 100 us  [on_device(): g_now = lax.all_to_all(f_now, 'head', 0, 0)]
    all_gather x1 -> x0, waiting for transfers between devices: 53.6 us -> none  [on_device(): residual_full = lax.all_gather(residual, 'head', axis=1, tiled=True)]
  transfers between devices with their start and end apart: 4 -> 3, of which waited for: 4 -> 3; matrix products, arithmetic and copies ran while one was open for 9% -> 8% of each run, Pallas kernels for 0% -> 0%
where the time goes in v1:
time: 334 us; the launch traced here: 333 us
  blocking collectives  160 us (48%)
  waiting for transfers between devices  113 us (34%)
  matrix products  29.1 us (9%)
  between operations  14.1 us (4%)
  local copies, waits for them, and re-layouts  10.4 us (3%)
  other arithmetic  6.88 us (2%)
    all_to_all x1, blocking collectives, on_device(): g_now = lax.all_to_all(f_now, 'head', 0, 0)  100 us
    all_gather x6, blocking collectives, entering(): pieces = lax.all_gather(so_far.astype(jnp.bfloat16), axis)  59.3 us
    reduce_scatter x1, waiting for transfers between devices, on_device(): lax.psum_scatter(partial_out.astype(jnp.bfloat16), 'head', scatter_dimens...  55.2 us
    reduce_scatter x1, waiting for transfers between devices, on_device(): lax.psum_scatter((product * weight_factor).astype(jnp.bfloat16), SEQ, sca...  38.5 us
    all_gather x1, waiting for transfers between devices, on_device(): whole_weight = lax.all_gather(out_weight, SEQ, axis=0, tiled=True)  18.6 us
    dot_general x1, matrix products, on_device(): lax.dot_general(attended, whole_weight, (((1,), (1,)), ((), ())), preferr...  6.74 us
  transfers between devices with their start and end apart: 3, of which 3 were waited for; matrix products, arithmetic and copies ran while one was open for 8% of the time, Pallas kernels for 0%

profile of v1, /device:TPU:2, one launch (start us, length us, event | category | flops | bytes accessed | tf_op | source)
XLA Modules:
  0.0 333.2 jit_solution(11192329112444400963)
XLA Ops:
  7.2 0.0 all-gather.4.cloned.1.call-start
  7.2 0.7 all-gather.4.cloned.1.call-update
  7.9 0.0 reduce-scatter.3.cloned.1.call-start
  8.0 1.3 copy.104
  9.3 1.4 multiply_convert_fusion.2
  10.7 0.2 copy.77
  10.9 0.3 convolution_convert_fusion.3
  11.2 2.0 all-gather
  13.2 0.1 iota_compare_fusion
  13.3 12.8 %all_gather.28 = bf16[4,4,128,128]{3,2,1,0:T(8,128)(2,1)S(1)} all-gather(bf16[1,4,128,128]{3,2,1,0:T(8,128)(2,1)S(1)} %fusion.41), channel_id=1, replica_groups=mesh['seq_0'=4,'seq_1'=4,'seq_2'=2,'head'=8] {'seq_1'}, dimensions={0}, use_global_device_ids=true | all-gather | bytes 655360 | tf_op jit(solution)/shard_map/all_gather | solution.py:23
  26.2 0.1 fusion.40
  26.2 15.3 %all_gather.29 = bf16[4,4,128,128]{3,2,1,0:T(8,128)(2,1)S(1)} all-gather(bf16[1,4,128,128]{3,2,1,0:T(8,128)(2,1)S(1)} %fusion.40), channel_id=1, replica_groups=mesh['seq_0'=4,'seq_1'=4,'seq_2'=2,'head'=8] {'seq_0'}, dimensions={0}, use_global_device_ids=true | all-gather | bytes 655360 | tf_op jit(solution)/shard_map/all_gather | solution.py:23
  41.6 0.3 fusion.20
  41.8 2.0 select_convert_fusion.1
  43.8 0.8 convolution_bitcast_fusion.1
  44.7 1.4 fusion
  46.1 18.6 %all-gather.4.cloned.1.call-done = bf16[4096,512]{1,0:T(8,128)(2,1)} async-done(((bf16[128,512]{1,0:T(8,128)(2,1)}), bf16[4096,512]{1,0:T(8,128)(2,1)}) %all-gather.4.cloned.1.call-update) | async-done | bytes 4194320 | tf_op jit(solution)/shard_map/all_gather | solution.py:70
  64.7 6.7 %convolution_convert_fusion = bf16[512,4096]{1,0:T(8,128)(2,1)} fusion(bf16[512,512]{0,1:T(8,128)(2,1)} %bitcast.119, bf16[4096,512]{1,0:T(8,128)(2,1)} %all-gather.4.cloned.1.call-done), kind=kOutput, calls=%fused_computation.1 | convolution fusion | flops 2149580800 | bytes 8912896 | tf_op jit(solution)/shard_map/dot_general | solution.py:71
  71.5 0.0 reduce-scatter.3.cloned.1.call-update
  71.5 0.0 reduce-scatter.5.cloned.1.call-start
  71.5 55.2 %reduce-scatter.3.cloned.1.call-done = bf16[512,512]{1,0:T(8,128)(2,1)} async-done(((bf16[512,4096]{1,0:T(8,128)(2,1)}), bf16[512,512]{1,0:T(8,128)(2,1)}) %reduce-scatter.3.cloned.1.call-update) | async-done | bytes 524304 | tf_op jit(solution)/shard_map/reduce_scatter | solution.py:74
  126.7 2.1 subtract_convert_fusion
  128.9 2.0 copy.58
  130.9 1.4 stack.2
  132.3 100.3 %all_to_all.5 = bf16[8,512,512]{1,2,0:T(8,128)(2,1)S(1)} all-to-all(bf16[8,512,512]{1,2,0:T(8,128)(2,1)S(1)} %stack.2), channel_id=1, replica_groups=mesh['seq_0'=4,'seq_1'=4,'seq_2'=2,'head'=8] {'head'}, dimensions={0} | all-to-all | bytes 8388608 | tf_op jit(solution)/shard_map/all_to_all | solution.py:79
  232.7 2.0 copy-done.3
  234.6 4.4 %multiply_convert_fusion = bf16[4096,512]{1,0:T(8,128)(2,1)} fusion(bf16[512,4096]{0,1:T(8,128)(2,1)S(1)} %bitcast.112, bf16[512,512]{0,1:T(8,128)(2,1)S(1)} %bitcast.120), kind=kOutput, calls=%fused_computation | convolution fusion | flops 2151677952 | bytes 8912896 | tf_op jit(solution)/shard_map/dot_general | solution.py:85
  239.1 0.0 reduce-scatter.5.cloned.1.call-update
  239.1 5.8 %convolution_convert_fusion.1 = bf16[512,512]{0,1:T(8,128)(2,1)S(1)} fusion(bf16[512,4096]{0,1:T(8,128)(2,1)} %bitcast.113, bf16[4096,512]{1,0:T(8,128)(2,1)} %all-gather.4.cloned.1.call-done), kind=kOutput, calls=%fused_computation.10 | convolution fusion | flops 2147745792 | bytes 8912896 | tf_op jit(solution)/shard_map/dot_general | solution.py:81
  245.0 0.3 convolution_convert_fusion.2
  245.3 2.3 all-gather.1
  247.7 13.5 %all_gather.32 = bf16[4,4,128,128]{3,2,1,0:T(8,128)(2,1)S(1)} all-gather(bf16[1,4,128,128]{3,2,1,0:T(8,128)(2,1)S(1)} %fusion.42), channel_id=1, replica_groups=mesh['seq_0'=4,'seq_1'=4,'seq_2'=2,'head'=8] {'seq_1'}, dimensions={0}, use_global_device_ids=true | all-gather | bytes 655360 | tf_op jit(solution)/shard_map/all_gather | solution.py:23
  261.2 0.1 fusion.39
  261.3 13.3 %all_gather.33 = bf16[4,4,128,128]{3,2,1,0:T(8,128)(2,1)S(1)} all-gather(bf16[1,4,128,128]{3,2,1,0:T(8,128)(2,1)S(1)} %fusion.39), channel_id=1, replica_groups=mesh['seq_0'=4,'seq_1'=4,'seq_2'=2,'head'=8] {'seq_0'}, dimensions={0}, use_global_device_ids=true | all-gather | bytes 655360 | tf_op jit(solution)/shard_map/all_gather | solution.py:23
  274.6 0.3 fusion.29
  274.8 0.4 fusion.44
  275.3 0.6 fusion.2
  275.9 1.0 copy.71
  276.9 1.9 select_convert_fusion
  278.9 0.4 fusion.43
  279.3 1.4 fusion.1
  280.7 2.1 copy.70
  282.8 1.8 convolution_bitcast_fusion
  284.7 0.6 convolution_add_fusion.2
  285.3 0.3 copy.63
  285.6 0.9 multiply_convert_fusion.1
  286.5 38.5 %reduce-scatter.5.cloned.1.call-done = bf16[128,512]{1,0:T(8,128)(2,1)} async-done(((bf16[4096,512]{1,0:T(8,128)(2,1)}), bf16[128,512]{1,0:T(8,128)(2,1)}) %reduce-scatter.5.cloned.1.call-update) | async-done | bytes 131088 | tf_op jit(solution)/shard_map/reduce_scatter | solution.py:88
  325.1 1.6 convert_element_type.247
  (22 shorter events, 0.1 us)
Async XLA Ops:
  7.2 3.7 %copy-start = (bf16[512,512]{1,0:T(8,128)(2,1)S(1)}, bf16[512,512]{1,0:T(8,128)(2,1)}, u32[]{:S(2)}) copy-start(bf16[512,512]{1,0:T(8,128)(2,1)} %param.7) | copy-start | bytes 1572868
  7.2 57.6 %all-gather.4.cloned.1.call-start = ((), (), s32[]{:S(2)}) async-start(), calls=%async_computation.3 | async-start | bytes 4325376 | tf_op jit(solution)/shard_map/all_gather | solution.py:70
  7.9 118.8 %reduce-scatter.3.cloned.1.call-start = ((), (), s32[]{:S(2)}) async-start(), calls=%async_computation.4 | async-start | bytes 4718592 | tf_op jit(solution)/shard_map/reduce_scatter | solution.py:74
  9.2 32.6 %copy-start.6 = (bf16[512,512]{0,1:T(8,128)(2,1)}, bf16[512,512]{0,1:T(8,128)(2,1)S(1)}, u32[]{:S(2)}) copy-start(bf16[512,512]{0,1:T(8,128)(2,1)S(1)} %copy.104) | copy-start | bytes 1572868
  13.3 31.4 %copy-start.9 = (pred[512,512]{1,0:T(8,128)(4,1)}, pred[512,512]{1,0:T(8,128)(4,1)S(1)}, u32[]{:S(2)}) copy-start(pred[512,512]{1,0:T(8,128)(4,1)S(1)} %iota_compare_fusion) | copy-start | bytes 786436
  41.8 2.8 copy-start.4
  71.5 253.6 %reduce-scatter.5.cloned.1.call-start = ((), (), s32[]{:S(2)}) async-start(), calls=%async_computation.5 | async-start | bytes 4325376 | tf_op jit(solution)/shard_map/reduce_scatter | solution.py:88
  132.3 102.3 %copy-start.8 = (bf16[4,128,512]{2,1,0:T(8,128)(2,1)S(1)}, bf16[4,128,512]{2,1,0:T(8,128)(2,1)}, u32[]{:S(2)}) copy-start(bf16[4,128,512]{2,1,0:T(8,128)(2,1)} %fusion) | copy-start | bytes 1572868
  232.7 2.0 copy-start.3
  245.0 30.3 %copy-start.1 = (bf16[512,512]{0,1:T(8,128)(2,1)}, bf16[512,512]{0,1:T(8,128)(2,1)S(1)}, u32[]{:S(2)}) copy-start(bf16[512,512]{0,1:T(8,128)(2,1)S(1)} %convolution_convert_fusion.1) | copy-start | bytes 1572868
  245.3 30.0 %copy-start.7 = (bf16[512,512]{1,0:T(8,128)(2,1)S(1)}, bf16[512,512]{1,0:T(8,128)(2,1)}, u32[]{:S(2)}) copy-start(bf16[512,512]{1,0:T(8,128)(2,1)} %param.6) | copy-start | bytes 1572868
  279.3 5.3 %copy-start.2 = (bf16[512,512]{0,1:T(8,128)(2,1)S(1)}, bf16[512,512]{0,1:T(8,128)(2,1)}, u32[]{:S(2)}) copy-start(bf16[512,512]{0,1:T(8,128)(2,1)} %copy-done.1) | copy-start | bytes 1572868
  280.7 4.0 %copy-start.5 = (f32[4,128,128]{2,1,0:T(8,128)S(1)}, f32[4,128,128]{2,1,0:T(8,128)}, u32[]{:S(2)}) copy-start(f32[4,128,128]{2,1,0:T(8,128)} %copy-done.4) | copy-start | bytes 786436
Sparse Core Ops, SparseCore 0:
  10.5 54.1 all-gather.3
  71.6 55.0 reduce-scatter.2
  239.2 85.7 reduce-scatter.4
